TPU v7x, 512 devices: a whole 4x4x16 slice. The times are simulated.
512 devices in a mesh: frames: 8 (over x_hi, y), queries: 64 (over x_lo, z, core).
Axes of the slice: x: 4 (x_hi: 2, x_lo: 2; x = x_hi * 2 + x_lo), y: 4, z: 16, core: 2. Of those that a mesh axis runs over, the one named last changes fastest.
Arguments:
- frame_maps: bfloat16 [16, 4096, 256], P('frames', 'queries'), may hold values from -6 to 6
- query_table: bfloat16 [8, 4096, 256], P('frames', 'queries'), may hold values from -6 to 6
- start_frame: int32 [4096], P('queries'), may hold values from 0 to 15
- row_ids: int32 [4096], P('queries'), may hold values from 0 to 63
- conv1_w: bfloat16 [3, 3, 1, 16], replicated, may hold values from -2 to 2
- conv1_b: float32 [16], replicated, may hold values from -3 to 3
- conv2_w: bfloat16 [3, 3, 16, 32], replicated, may hold values from -0.5 to 0.5
- conv2_b: float32 [32], replicated, may hold values from -3 to 3
- proj_w: bfloat16 [32, 512], replicated, may hold values from -1 to 1
- proj_b: float32 [512], replicated, may hold values from -3 to 3
- time_w: float32 [3, 512], replicated, may hold values from -3 to 3
- time_b: float32 [512], replicated, may hold values from -3 to 3
Outputs:
- track_feats: bfloat16 [4096, 16, 512], P('queries', 'frames')
Inputs may be any that keep to these rules, and one draw needn't show every extreme that they name: `start_frame`: the frame in which the query was picked, one of the 16 frames. `row_ids`: a row index within the query's own block of 64 rows.
All inputs are finite; a program needn't handle non-finite values.
Results may differ from a plain program's by a relative error of at most 0.001.
The roundings to bfloat16 on the way count: a program that leaves them out, or rounds other values in their place, can miss the bound.
Values may be sent and summed in bfloat16 or wider, within the bound.
No kernel may reach another device: no remote copies, remote signals or barrier semaphores. Data moves between devices by JAX's collectives and lax.ppermute only.
A program may use at most 64 MiB of HBM per device.

v0:
```python
import jax
import jax.numpy as jnp
from jax import lax
from jax.sharding import PartitionSpec as P

MAP = 64
CH2 = 32


def padded(block, sides, width):
    for axis, dim in sides:
        count = lax.axis_size(axis)
        forward = [(i, i + 1) for i in range(count - 1)]
        backward = [(target, source) for source, target in forward]
        low = lax.ppermute(
            lax.slice_in_dim(block, block.shape[dim] - width, None, axis=dim), axis, forward
        )
        high = lax.ppermute(lax.slice_in_dim(block, 0, width, axis=dim), axis, backward)
        block = jnp.concatenate([low, block, high], axis=dim)
    return block


def per_device(
    frame_maps,
    query_table,
    start_frame,
    row_ids,
    conv1_w,
    conv1_b,
    conv2_w,
    conv2_b,
    proj_w,
    proj_b,
    time_w,
    time_b,
):
    frames_here = frame_maps.shape[0]
    frame_block = lax.axis_index("frames")
    own_rows = query_table[0][row_ids]
    owned = start_frame // frames_here == frame_block
    own_term = jnp.where(owned[:, None], own_rows.astype(jnp.float32), 0.0)
    queries = lax.psum(own_term.astype(jnp.bfloat16), "frames")
    query_count = queries.shape[0]
    every_query = lax.all_gather(queries, "queries", axis=0, tiled=True)
    band = (
        jnp.einsum("frc,qc->rfq", frame_maps, every_query, preferred_element_type=jnp.float32)
        * 0.0625
    ).astype(jnp.bfloat16)
    costs = lax.all_to_all(band, "queries", split_axis=2, concat_axis=0, tiled=True)
    block_size = min(64, query_count)
    block_count = query_count // block_size
    pooled_init = jnp.zeros((CH2, frames_here, query_count), jnp.bfloat16)

    def one_block(block_index, pooled_acc):
        images = costs.reshape(MAP, MAP, 1, frames_here * block_size)
        layer_one = lax.conv_general_dilated(
            images,
            conv1_w,
            (2, 2),
            ((1, 1), (1, 1)),
            dimension_numbers=("HWCN", "HWIO", "HWCN"),
            preferred_element_type=jnp.float32,
        )
        layer_one = jax.nn.relu(layer_one + conv1_b[None, None, :, None]).astype(jnp.bfloat16)
        layer_two = lax.conv_general_dilated(
            layer_one,
            conv2_w,
            (2, 2),
            ((1, 1), (1, 1)),
            dimension_numbers=("HWCN", "HWIO", "HWCN"),
            preferred_element_type=jnp.float32,
        )
        layer_two = jax.nn.relu(layer_two + conv2_b[None, None, :, None])
        pooled_block = (
            jnp.mean(layer_two, axis=(0, 1))
            .astype(jnp.bfloat16)
            .reshape(CH2, frames_here, block_size)
        )
        return pooled_block

    pooled = lax.fori_loop(0, block_count, one_block, pooled_init)
    projected = padded(
        (
            jnp.einsum("cfq,cd->qfd", pooled, proj_w, preferred_element_type=jnp.float32) + proj_b
        ).astype(jnp.bfloat16),
        (("frames", 1),),
        1,
    )
    widened_f32 = projected.astype(jnp.float32)
    mixed = (
        time_w[0] * widened_f32[:, :-2]
        + time_w[1] * widened_f32[:, 1:-1]
        + time_w[2] * widened_f32[:, 2:]
        + time_b
    )
    return mixed.astype(jnp.bfloat16)


def solution(mesh):
    placed = (
        P("frames", "queries", None),
        P("frames", "queries", None),
        P("queries"),
        P("queries"),
        P(),
        P(),
        P(),
        P(),
        P(),
        P(),
        P(),
        P(),
    )
    return jax.shard_map(
        per_device,
        mesh=mesh,
        in_specs=placed,
        out_specs=P("queries", "frames", None),
        check_vma=False,
    )
```

profile of v0, /device:TPU:57, one launch (start us, length us, event | category | flops | bytes accessed | tf_op | source)
XLA Modules:
  0.0 289.6 jit_solution(6858478085503585251)
XLA Ops:
  6.5 0.0 copy-start
  6.5 0.0 all-gather.2.cloned.1.call-start
  6.5 0.7 compare_select_fusion
  7.2 1.4 gather_fusion
  8.7 0.7 fusion.18
  9.3 0.1 select_convert_fusion
  9.4 29.9 %psum.7 = bf16[64,256]{1,0:T(8,128)(2,1)} all-reduce(bf16[64,256]{1,0:T(8,128)(2,1)S(1)} %select_convert_fusion), channel_id=1, replica_groups=mesh['frames'=8,'queries'=64] {'frames'}, use_global_device_ids=true, to_apply=%region_0.1 | all-reduce | flops 16384 | bytes 65536 | tf_op jit(solution)/shard_map/psum | solution.py:42
  39.3 0.0 all-gather.2.cloned.1.call-update
  39.4 134.6 %all-gather.2.cloned.1.call-done = bf16[4096,256]{1,0:T(8,128)(2,1)} async-done(((bf16[64,256]{1,0:T(8,128)(2,1)}), bf16[4096,256]{1,0:T(8,128)(2,1)}) %all-gather.2.cloned.1.call-update) | async-done | bytes 2097168 | tf_op jit(solution)/shard_map/all_gather | solution.py:44
  174.0 0.0 copy-done
  174.0 2.4 fusion.1
  176.4 2.8 copy.21
  179.2 1.5 reshape.32
  180.7 63.0 %all_to_all.15 = bf16[64,2,4096]{2,1,0:T(2,128)(2,1)} all-to-all(bf16[64,2,4096]{2,1,0:T(2,128)(2,1)S(1)} %reshape.32), channel_id=1, replica_groups=mesh['frames'=8,'queries'=64] {'queries'}, dimensions={0} | all-to-all | bytes 2097152 | tf_op jit(solution)/shard_map/all_to_all | solution.py:49
  243.8 5.1 %reshape.33 = bf16[4096,2,64]{2,1,0:T(2,128)(2,1)S(1)} reshape(bf16[64,2,4096]{2,1,0:T(2,128)(2,1)} %all_to_all.15) | data formatting | bytes 2097152
  248.8 6.4 %copy.22 = bf16[64,2,64,64]{3,1,0,2:T(2,128)(2,1)} copy(bf16[64,2,64,64]{0,1,3,2:T(2,128)(2,1)S(1)} %bitcast.22) | data formatting | bytes 2097152 | tf_op jit(solution)/shard_map/all_to_all | solution.py:49
  255.3 0.0 copy-start.5
  255.3 0.0 copy-start.6
  255.3 0.0 copy-start.7
  255.3 0.0 copy-start.8
  255.3 7.8 %reshape.31 = bf16[64,64,1,128]{3,2,1,0:T(2,128)(2,1)S(1)} reshape(bf16[64,64,2,64]{3,2,1,0:T(2,128)(2,1)} %bitcast.23) | data formatting | bytes 2097152 | tf_op jit(solution)/shard_map/while/body/eval_jaxpr/reshape | solution.py:55
  263.1 0.0 copy-done.5
  263.1 0.0 copy-done.6
  263.1 0.0 copy-done.7
  263.1 0.0 copy-done.8
  263.1 0.0 copy-start.1
  263.1 0.0 copy-start.3
  263.1 0.0 copy-start.2
  263.2 0.0 copy-start.4
  263.2 5.5 %maximum_reduce_fusion = f32[32,128]{1,0:T(8,128)S(1)} fusion(f32[32]{0:T(128)S(1)} %copy-done.7, bf16[3,3,16,32]{3,2,1,0:T(8,128)(2,1)S(1)} %copy-done.5, f32[16]{0:T(128)S(1)} %copy-done.8, bf16[64,64,1,128]{3,2,1,0:T(2,128)(2,1)S(1)} %reshape.31, bf16[3,3,1,16]{3,1,2,0:T(4,128)(2,1)S(1)} %copy-done.6), kind=kOutput, calls=%fused_computation.6 | convolution fusion | flops 335937536 | bytes 1074656 | tf_op jit(solution)/shard_map/while/body/eval_jaxpr/conv_general_dilated | solution.py:65
  268.7 0.1 convert_element_type.42
  268.7 0.0 copy-done.1
  268.7 0.0 copy-done.3
  268.7 0.2 fusion.9
  269.0 4.2 %collective-permute-start = (bf16[64,1,512]{2,0,1:T(8,128)(2,1)S(1)}, bf16[64,1,512]{2,0,1:T(8,128)(2,1)S(1)}, u32[]{:S(2)}, u32[]{:S(2)}) collective-permute-start(bf16[64,1,512]{2,0,1:T(8,128)(2,1)S(1)} %get-tuple-element.16), channel_id=1, source_target_pairs={{0,64},{64,128},{128,192},{192,256},{256,320},{320,384},{384,448},... | collective-permute-start | bytes 196616 | tf_op jit(solution)/shard_map/ppermute | solution.py:15
  273.2 1.9 collective-permute-start.1
  275.2 0.0 copy-done.2
  275.2 0.0 collective-permute-done
  275.2 6.7 %collective-permute-done.1 = bf16[64,1,512]{2,0,1:T(8,128)(2,1)S(1)} collective-permute-done((bf16[64,1,512]{2,0,1:T(8,128)(2,1)S(1)}, bf16[64,1,512]{2,0,1:T(8,128)(2,1)S(1)}, u32[]{:S(2)}, u32[]{:S(2)}) %collective-permute-start.1) | collective-permute-done | bytes 65568 | tf_op jit(solution)/shard_map/ppermute | solution.py:18
  281.9 0.0 copy-done.4
  281.9 0.1 fusion.12
  282.0 0.8 copy.26
  (5 shorter events, 0.1 us)
Async XLA Ops:
  6.5 167.4 %copy-start = (bf16[2,64,256]{2,1,0:T(8,128)(2,1)S(1)}, bf16[2,64,256]{2,1,0:T(8,128)(2,1)}, u32[]{:S(2)}) copy-start(bf16[2,64,256]{2,1,0:T(8,128)(2,1)} %param.12) | copy-start | bytes 196612
  6.5 167.4 %all-gather.2.cloned.1.call-start = ((), (), s32[]{:S(2)}) async-start(), calls=%async_computation.1 | async-start | bytes 2129920 | tf_op jit(solution)/shard_map/all_gather | solution.py:44
  255.3 7.8 %copy-start.5 = (bf16[3,3,16,32]{3,2,1,0:T(8,128)(2,1)S(1)}, bf16[3,3,16,32]{3,2,1,0:T(8,128)(2,1)}, u32[]{:S(2)}) copy-start(bf16[3,3,16,32]{3,2,1,0:T(8,128)(2,1)} %param.18) | copy-start | bytes 27652
  255.3 7.8 %copy-start.6 = (bf16[3,3,1,16]{3,1,2,0:T(4,128)(2,1)S(1)}, bf16[3,3,1,16]{3,1,2,0:T(4,128)(2,1)}, u32[]{:S(2)}) copy-start(bf16[3,3,1,16]{3,1,2,0:T(4,128)(2,1)} %param.16) | copy-start | bytes 868
  255.3 7.8 %copy-start.7 = (f32[32]{0:T(128)S(1)}, f32[32]{0:T(128)}, u32[]{:S(2)}) copy-start(f32[32]{0:T(128)} %param.19) | copy-start | bytes 388
  255.3 7.8 %copy-start.8 = (f32[16]{0:T(128)S(1)}, f32[16]{0:T(128)}, u32[]{:S(2)}) copy-start(f32[16]{0:T(128)} %param.17) | copy-start | bytes 196
  263.1 5.6 %copy-start.1 = (bf16[32,512]{1,0:T(8,128)(2,1)S(1)}, bf16[32,512]{1,0:T(8,128)(2,1)}, u32[]{:S(2)}) copy-start(bf16[32,512]{1,0:T(8,128)(2,1)} %param.20) | copy-start | bytes 98308
  263.1 5.6 %copy-start.3 = (f32[512]{0:T(512)S(1)}, f32[512]{0:T(512)}, u32[]{:S(2)}) copy-start(f32[512]{0:T(512)} %param.21) | copy-start | bytes 6148
  263.1 12.0 %copy-start.2 = (f32[3,512]{1,0:T(4,128)S(1)}, f32[3,512]{1,0:T(4,128)}, u32[]{:S(2)}) copy-start(f32[3,512]{1,0:T(4,128)} %param.22) | copy-start | bytes 18436
  263.2 18.8 %copy-start.4 = (f32[512]{0:T(512)S(1)}, f32[512]{0:T(512)}, u32[]{:S(2)}) copy-start(f32[512]{0:T(512)} %param.23) | copy-start | bytes 6148
  269.0 6.2 %collective-permute-start = (bf16[64,1,512]{2,0,1:T(8,128)(2,1)S(1)}, bf16[64,1,512]{2,0,1:T(8,128)(2,1)S(1)}, u32[]{:S(2)}, u32[]{:S(2)}) collective-permute-start(bf16[64,1,512]{2,0,1:T(8,128)(2,1)S(1)} %get-tuple-element.16), channel_id=1, source_target_pairs={{0,64},{64,128},{128,192},{192,256},{256,320},{320,384},{384,448},... | collective-permute-start | bytes 196616 | tf_op jit(solution)/shard_map/ppermute | solution.py:15
  273.2 8.6 %collective-permute-start.1 = (bf16[64,1,512]{2,0,1:T(8,128)(2,1)S(1)}, bf16[64,1,512]{2,0,1:T(8,128)(2,1)S(1)}, u32[]{:S(2)}, u32[]{:S(2)}) collective-permute-start(bf16[64,1,512]{2,0,1:T(8,128)(2,1)S(1)} %get-tuple-element.17), channel_id=1, source_target_pairs={{64,0},{128,64},{192,128},{256,192},{320,256},{384,320},{448,384},... | collective-permute-start | bytes 196616 | tf_op jit(solution)/shard_map/ppermute | solution.py:18
Sparse Core Ops, SparseCore 0:
  39.5 134.4 all-gather.1
where the time goes:
time: 290 us
  waiting for transfers between devices  141 us (49%)
  blocking collectives  93 us (32%)
  local copies, waits for them, and re-layouts  26 us (9%)
  between operations  13.6 us (5%)
  matrix products  8.08 us (3%)
  starting transfers between devices  6.17 us (2%)
    all_gather x1, waiting for transfers between devices, per_device(): every_query = lax.all_gather(queries, 'queries', axis=0, tiled=True)  135 us
    all_to_all x1, blocking collectives, per_device(): lax.all_to_all(band, 'queries', split_axis=2, concat_axis=0, tiled=True)  63 us
    psum x1, blocking collectives, per_device(): queries = lax.psum(own_term.astype(jnp.bfloat16), 'frames')  29.9 us
    reshape x1, local copies, waits for them, and re-layouts, one_block(): images = costs.reshape(MAP, MAP, 1, frames_here * block_size)  7.79 us
    ppermute x1, waiting for transfers between devices, padded(): lax.ppermute(lax.slice_in_dim(block, 0, width, axis=dim), axis, backward)  6.66 us
    unnamed x20, local copies, waits for them, and re-layouts  6.6 us
    all_to_all x1, local copies, waits for them, and re-layouts, per_device(): lax.all_to_all(band, 'queries', split_axis=2, concat_axis=0, tiled=True)  6.44 us
  transfers between devices with their start and end apart: 3, of which 2 were waited for; matrix products, arithmetic and copies ran while one was open for 0% of the time, Pallas kernels for 0%

commit v1 on v0

--- a/solution.py
+++ b/solution.py
@@ -41,7 +41,8 @@
     own_term = jnp.where(owned[:, None], own_rows.astype(jnp.float32), 0.0)
     queries = lax.psum(own_term.astype(jnp.bfloat16), "frames")
     query_count = queries.shape[0]
-    every_query = lax.all_gather(queries, "queries", axis=0, tiled=True)
+    repeated = jnp.stack([queries] * lax.axis_size("queries"))
+    every_query = jnp.concatenate(lax.all_to_all(repeated, "queries", 0, 0), axis=0)
     band = (
         jnp.einsum("frc,qc->rfq", frame_maps, every_query, preferred_element_type=jnp.float32)
         * 0.0625

time: 290 us -> 264 us (0.910)
  waiting for transfers between devices: 141 us -> 6.66 us
  blocking collectives: 93 us -> 212 us
  between operations: 13.6 us -> 0.2 us
  starting transfers between devices: 6.17 us -> 10 us
    all_gather x1 -> x0, waiting for transfers between devices: 135 us -> none  [per_device(): every_query = lax.all_gather(queries, 'queries', axis=0, tiled=True)]
    all_to_all x0 -> x1, blocking collectives: none -> 122 us  [per_device(): lax.all_to_all(repeated, 'queries', 0, 0)]
    ppermute x1, starting transfers between devices: 4.24 us -> 8.13 us  [padded(): lax.ppermute(lax.slice_in_dim(block, block.shape[dim] - width, None, axis...]
  transfers between devices with their start and end apart: 3 -> 2, of which waited for: 2 -> 1; matrix products, arithmetic and copies ran while one was open for 0% -> 0% of each run, Pallas kernels for 0% -> 0%
where the time goes in v1:
time: 264 us; the launch traced here: 263 us
  blocking collectives  212 us (80%)
  local copies, waits for them, and re-layouts  26.2 us (10%)
  starting transfers between devices  10 us (4%)
  waiting for transfers between devices  6.66 us (3%)
  matrix products  6.5 us (2%)
    all_to_all x1, blocking collectives, per_device(): lax.all_to_all(repeated, 'queries', 0, 0)  122 us
    all_to_all x1, blocking collectives, per_device(): lax.all_to_all(band, 'queries', split_axis=2, concat_axis=0, tiled=True)  61.2 us
    psum x1, blocking collectives, per_device(): queries = lax.psum(own_term.astype(jnp.bfloat16), 'frames')  29.3 us
    ppermute x1, starting transfers between devices, padded(): lax.ppermute(lax.slice_in_dim(block, block.shape[dim] - width, None, axis...  8.13 us
    reshape x1, local copies, waits for them, and re-layouts, one_block(): images = costs.reshape(MAP, MAP, 1, frames_here * block_size)  7.79 us
    ppermute x1, waiting for transfers between devices, padded(): lax.ppermute(lax.slice_in_dim(block, 0, width, axis=dim), axis, backward)  6.66 us
    unnamed x20, local copies, waits for them, and re-layouts  6.6 us
    all_to_all x1, local copies, waits for them, and re-layouts, per_device(): lax.all_to_all(band, 'queries', split_axis=2, concat_axis=0, tiled=True)  6.43 us
  transfers between devices with their start and end apart: 2, of which 1 were waited for; matrix products, arithmetic and copies ran while one was open for 0% of the time, Pallas kernels for 0%

profile of v1, /device:TPU:57, one launch (start us, length us, event | category | flops | bytes accessed | tf_op | source)
XLA Modules:
  0.0 263.3 jit_solution(15751702252090498787)
XLA Ops:
  0.0 0.0 copy-start
  0.0 0.7 compare_select_fusion
  0.7 1.4 gather_fusion
  2.1 0.7 fusion.17
  2.8 0.1 select_convert_fusion
  2.9 29.3 %psum.7 = bf16[64,256]{1,0:T(8,128)(2,1)S(1)} all-reduce(bf16[64,256]{1,0:T(8,128)(2,1)S(1)} %select_convert_fusion), channel_id=1, replica_groups=mesh['frames'=8,'queries'=64] {'frames'}, use_global_device_ids=true, to_apply=%region_0.1 | all-reduce | flops 16384 | bytes 65536 | tf_op jit(solution)/shard_map/psum | solution.py:42
  32.2 0.2 stack.2
  32.4 121.6 %all_to_all.20 = bf16[64,64,256]{2,1,0:T(8,128)(2,1)S(1)} all-to-all(bf16[64,64,256]{2,1,0:T(8,128)(2,1)S(1)} %stack.2), channel_id=1, replica_groups=mesh['frames'=8,'queries'=64] {'queries'}, dimensions={0} | all-to-all | bytes 4194304 | tf_op jit(solution)/shard_map/all_to_all | solution.py:45
  154.0 0.0 copy-done
  154.0 0.8 fusion.1
  154.8 2.8 %copy.21 = bf16[64,2,4096]{0,1,2:T(2,128)(2,1)S(1)} copy(bf16[64,2,4096]{2,0,1:T(8,128)(2,1)S(1)} %fusion.1) | data formatting | bytes 2097152 | tf_op jit(solution)/shard_map/convert_element_type | solution.py:49
  157.7 1.5 reshape.38
  159.2 61.2 %all_to_all.21 = bf16[64,2,4096]{2,1,0:T(2,128)(2,1)} all-to-all(bf16[64,2,4096]{2,1,0:T(2,128)(2,1)S(1)} %reshape.38), channel_id=1, replica_groups=mesh['frames'=8,'queries'=64] {'queries'}, dimensions={0} | all-to-all | bytes 2097152 | tf_op jit(solution)/shard_map/all_to_all | solution.py:50
  220.4 5.1 %reshape.39 = bf16[4096,2,64]{2,1,0:T(2,128)(2,1)S(1)} reshape(bf16[64,2,4096]{2,1,0:T(2,128)(2,1)} %all_to_all.21) | data formatting | bytes 2097152
  225.5 6.4 %copy.22 = bf16[64,2,64,64]{3,1,0,2:T(2,128)(2,1)} copy(bf16[64,2,64,64]{0,1,3,2:T(2,128)(2,1)S(1)} %bitcast.23) | data formatting | bytes 2097152 | tf_op jit(solution)/shard_map/all_to_all | solution.py:50
  231.9 0.0 copy-start.5
  231.9 0.0 copy-start.6
  231.9 0.0 copy-start.7
  231.9 0.0 copy-start.8
  231.9 7.8 %reshape.37 = bf16[64,64,1,128]{3,2,1,0:T(2,128)(2,1)S(1)} reshape(bf16[64,64,2,64]{3,2,1,0:T(2,128)(2,1)} %bitcast.24) | data formatting | bytes 2097152 | tf_op jit(solution)/shard_map/while/body/eval_jaxpr/reshape | solution.py:56
  239.7 0.0 copy-done.5
  239.7 0.0 copy-done.6
  239.7 0.0 copy-done.7
  239.7 0.0 copy-done.8
  239.7 0.0 copy-start.1
  239.7 0.0 copy-start.3
  239.7 0.0 copy-start.2
  239.7 0.0 copy-start.4
  239.8 5.5 %maximum_reduce_fusion = f32[32,128]{1,0:T(8,128)S(1)} fusion(f32[32]{0:T(128)S(1)} %copy-done.7, bf16[3,3,16,32]{3,2,1,0:T(8,128)(2,1)S(1)} %copy-done.5, f32[16]{0:T(128)S(1)} %copy-done.8, bf16[64,64,1,128]{3,2,1,0:T(2,128)(2,1)S(1)} %reshape.37, bf16[3,3,1,16]{3,1,2,0:T(4,128)(2,1)S(1)} %copy-done.6), kind=kOutput, calls=%fused_computation.6 | convolution fusion | flops 335937536 | bytes 1074656 | tf_op jit(solution)/shard_map/while/body/eval_jaxpr/conv_general_dilated | solution.py:66
  245.2 0.1 convert_element_type.42
  245.3 0.0 copy-done.1
  245.3 0.0 copy-done.3
  245.3 0.2 fusion.8
  245.6 8.1 %collective-permute-start = (bf16[64,1,512]{2,0,1:T(8,128)(2,1)S(1)}, bf16[64,1,512]{2,0,1:T(8,128)(2,1)S(1)}, u32[]{:S(2)}, u32[]{:S(2)}) collective-permute-start(bf16[64,1,512]{2,0,1:T(8,128)(2,1)S(1)} %get-tuple-element.16), channel_id=1, source_target_pairs={{0,64},{64,128},{128,192},{192,256},{256,320},{320,384},{384,448},... | collective-permute-start | bytes 196616 | tf_op jit(solution)/shard_map/ppermute | solution.py:15
  253.7 1.9 collective-permute-start.1
  255.6 0.0 copy-done.2
  255.7 0.0 collective-permute-done
  255.7 6.7 %collective-permute-done.1 = bf16[64,1,512]{2,0,1:T(8,128)(2,1)S(1)} collective-permute-done((bf16[64,1,512]{2,0,1:T(8,128)(2,1)S(1)}, bf16[64,1,512]{2,0,1:T(8,128)(2,1)S(1)}, u32[]{:S(2)}, u32[]{:S(2)}) %collective-permute-start.1) | collective-permute-done | bytes 65568 | tf_op jit(solution)/shard_map/ppermute | solution.py:18
  262.4 0.0 copy-done.4
  262.4 0.1 fusion.11
  262.5 0.8 copy.26
  (5 shorter events, 0.1 us)
Async XLA Ops:
  0.0 154.0 %copy-start = (bf16[2,64,256]{2,1,0:T(8,128)(2,1)S(1)}, bf16[2,64,256]{2,1,0:T(8,128)(2,1)}, u32[]{:S(2)}) copy-start(bf16[2,64,256]{2,1,0:T(8,128)(2,1)} %param.12) | copy-start | bytes 196612
  231.9 7.8 %copy-start.5 = (bf16[3,3,16,32]{3,2,1,0:T(8,128)(2,1)S(1)}, bf16[3,3,16,32]{3,2,1,0:T(8,128)(2,1)}, u32[]{:S(2)}) copy-start(bf16[3,3,16,32]{3,2,1,0:T(8,128)(2,1)} %param.18) | copy-start | bytes 27652
  231.9 7.8 %copy-start.6 = (bf16[3,3,1,16]{3,1,2,0:T(4,128)(2,1)S(1)}, bf16[3,3,1,16]{3,1,2,0:T(4,128)(2,1)}, u32[]{:S(2)}) copy-start(bf16[3,3,1,16]{3,1,2,0:T(4,128)(2,1)} %param.16) | copy-start | bytes 868
  231.9 7.8 %copy-start.7 = (f32[32]{0:T(128)S(1)}, f32[32]{0:T(128)}, u32[]{:S(2)}) copy-start(f32[32]{0:T(128)} %param.19) | copy-start | bytes 388
  231.9 7.8 %copy-start.8 = (f32[16]{0:T(128)S(1)}, f32[16]{0:T(128)}, u32[]{:S(2)}) copy-start(f32[16]{0:T(128)} %param.17) | copy-start | bytes 196
  239.7 5.6 %copy-start.1 = (bf16[32,512]{1,0:T(8,128)(2,1)S(1)}, bf16[32,512]{1,0:T(8,128)(2,1)}, u32[]{:S(2)}) copy-start(bf16[32,512]{1,0:T(8,128)(2,1)} %param.20) | copy-start | bytes 98308
  239.7 5.6 %copy-start.3 = (f32[512]{0:T(512)S(1)}, f32[512]{0:T(512)}, u32[]{:S(2)}) copy-start(f32[512]{0:T(512)} %param.21) | copy-start | bytes 6148
  239.7 15.9 %copy-start.2 = (f32[3,512]{1,0:T(4,128)S(1)}, f32[3,512]{1,0:T(4,128)}, u32[]{:S(2)}) copy-start(f32[3,512]{1,0:T(4,128)} %param.22) | copy-start | bytes 18436
  239.7 22.6 %copy-start.4 = (f32[512]{0:T(512)S(1)}, f32[512]{0:T(512)}, u32[]{:S(2)}) copy-start(f32[512]{0:T(512)} %param.23) | copy-start | bytes 6148
  245.6 10.1 %collective-permute-start = (bf16[64,1,512]{2,0,1:T(8,128)(2,1)S(1)}, bf16[64,1,512]{2,0,1:T(8,128)(2,1)S(1)}, u32[]{:S(2)}, u32[]{:S(2)}) collective-permute-start(bf16[64,1,512]{2,0,1:T(8,128)(2,1)S(1)} %get-tuple-element.16), channel_id=1, source_target_pairs={{0,64},{64,128},{128,192},{192,256},{256,320},{320,384},{384,448},... | collective-permute-start | bytes 196616 | tf_op jit(solution)/shard_map/ppermute | solution.py:15
  253.7 8.6 %collective-permute-start.1 = (bf16[64,1,512]{2,0,1:T(8,128)(2,1)S(1)}, bf16[64,1,512]{2,0,1:T(8,128)(2,1)S(1)}, u32[]{:S(2)}, u32[]{:S(2)}) collective-permute-start(bf16[64,1,512]{2,0,1:T(8,128)(2,1)S(1)} %get-tuple-element.17), channel_id=1, source_target_pairs={{64,0},{128,64},{192,128},{256,192},{320,256},{384,320},{448,384},... | collective-permute-start | bytes 196616 | tf_op jit(solution)/shard_map/ppermute | solution.py:18
